TPU v7x, 32 devices: a whole 2x2x4 slice. The times are simulated.
32 devices in a mesh: guide: 2 (over core), blk: 16 (over z, y, x).
Axes of the slice: x: 2, y: 2, z: 4, core: 2. Of those that a mesh axis runs over, the one named last changes fastest.
Arguments:
- x_cols: bfloat16 [128, 2048], P(None, 'blk'), may hold values from -3 to 3
- queries: bfloat16 [128, 9216], P('blk'), may hold values from -64 to 64
- new_kv: bfloat16 [128, 576], P('blk'), may hold values from -6 to 6
- cache: bfloat16 [2, 128, 256, 576], P('guide', 'blk'), may hold values from -8 to 8
- lengths: int32 [2, 128], P('guide'), may hold values from 2 to 256, as said below
- perm: int32 [128], replicated, may hold values from 0 to 127, each once
- guide_scale: float32 [128], replicated, may hold values from 1.5 to 7.5
- w_uv: bfloat16 [16, 512, 128], replicated, may hold values from -0.75 to 0.75
- w_out: bfloat16 [2048, 2048], P(None, 'blk'), may hold values from -0.125 to 0.125
- mlp_gain: float32 [2048], replicated, may hold values from 0.5 to 1.5
- w_gate: bfloat16 [2048, 10944], P(None, 'blk'), may hold values from -0.125 to 0.125
- w_up: bfloat16 [2048, 10944], P(None, 'blk'), may hold values from -0.125 to 0.125
- w_down: bfloat16 [10944, 2048], P('blk'), may hold values from -0.0546875 to 0.0546875
- head_gain: float32 [2048], replicated, may hold values from 0.5 to 1.5
- w_head: bfloat16 [2048, 102400], P(None, 'blk'), may hold values from -0.125 to 0.125
Outputs:
- guided: bfloat16 [128, 102400], P('guide', 'blk')
Inputs may be any that keep to these rules, and one draw needn't show every extreme that they name: Positions 0 to lengths[g, r] - 1 of request r's cache in group g are live; each group has a request with 256 live positions. Slot s holds request perm[s]; every request has one slot.
All inputs are finite; a program needn't handle non-finite values.
Results may differ from a plain program's by a relative error of at most 0.018.
Values may be sent and summed in bfloat16 or wider, within the bound.
No kernel may reach another device: no remote copies, remote signals or barrier semaphores. Data moves between devices by JAX's collectives and lax.ppermute only.
A program may use at most 128 MiB of HBM per device.

v0:
```python
import jax
import jax.numpy as jnp
from jax import lax
from jax.sharding import PartitionSpec as P

FF = 10944


def partner(value, axis, apart):
    mask = 2**apart
    pairs = [(source, source ^ mask) for source in range(lax.axis_size(axis))]
    return lax.ppermute(value, axis, pairs)


def rms_round(hidden, gain):
    values = hidden.astype(jnp.float32)
    meansq = jnp.mean(values * values, axis=-1, keepdims=True)
    return (values * lax.rsqrt(meansq + 1e-06) * gain).astype(jnp.bfloat16)


def body(
    x_cols,
    queries,
    new_kv,
    cache,
    lengths,
    perm,
    guide_scale,
    w_uv,
    w_out,
    mlp_gain,
    w_gate,
    w_up,
    w_down,
    head_gain,
    w_head,
):
    guide_index = lax.axis_index("guide")
    blk_index = lax.axis_index("blk")
    slots_dev = queries.shape[0]
    heads_count = w_uv.shape[0]
    latent_size = w_uv.shape[1]
    key_width = new_kv.shape[1]
    score_scale = (w_uv.shape[2] + key_width - latent_size) ** (-0.5)
    slot_ids = blk_index * slots_dev + jnp.arange(slots_dev, dtype=jnp.int32)
    owners = jnp.take(perm, slot_ids)
    live_len = jnp.take(lengths[0], owners)
    query_heads = queries.reshape(slots_dev, heads_count, key_width)
    cached_keys = cache[0]
    scores = (
        jnp.einsum("shk,slk->shl", query_heads, cached_keys, preferred_element_type=jnp.float32)
        * score_scale
    )
    own_score = (
        jnp.einsum("shk,sk->sh", query_heads, new_kv, preferred_element_type=jnp.float32)
        * score_scale
    )
    live_mask = (
        jnp.arange(cached_keys.shape[1], dtype=jnp.int32)[None, None, :] < live_len[:, None, None]
    )
    scores = jnp.where(live_mask, scores, jnp.float32(-1e30))
    peak_score = jnp.maximum(jnp.max(scores, axis=-1), own_score)
    probs = jnp.where(live_mask, jnp.exp(scores - peak_score[..., None]), jnp.float32(0.0))
    own_prob = jnp.exp(own_score - peak_score)
    softmax_total = jnp.sum(probs, axis=-1) + own_prob
    weights = (probs / softmax_total[..., None]).astype(jnp.bfloat16)
    own_weight = (own_prob / softmax_total).astype(jnp.bfloat16)
    latent_out = jnp.einsum(
        "shl,slc->shc", weights, cached_keys[:, :, :latent_size], preferred_element_type=jnp.float32
    )
    latent_out = latent_out + own_weight.astype(jnp.float32)[..., None] * new_kv[
        :, None, :latent_size
    ].astype(jnp.float32)
    value_rows = jnp.einsum(
        "shc,hcd->shd", latent_out.astype(jnp.bfloat16), w_uv, preferred_element_type=jnp.float32
    )
    value_rows = value_rows.astype(jnp.bfloat16).reshape(slots_dev, -1)
    attended = jnp.dot(
        lax.all_gather(value_rows, "blk", axis=0, tiled=True),
        w_out,
        preferred_element_type=jnp.float32,
    )
    residual = (x_cols.astype(jnp.float32) + attended).astype(jnp.bfloat16)
    rows_full = lax.all_gather(residual, "blk", axis=1, tiled=True)
    normed = rms_round(rows_full, mlp_gain)
    unit_count = w_gate.shape[1]
    gate_out = jnp.dot(normed, w_gate, preferred_element_type=jnp.float32)
    up_out = jnp.dot(normed, w_up, preferred_element_type=jnp.float32)
    unit_ids = blk_index * unit_count + jnp.arange(unit_count, dtype=jnp.int32)
    hidden = jnp.where(
        unit_ids[None, :] < FF, jax.nn.silu(gate_out) * up_out, jnp.float32(0.0)
    ).astype(jnp.bfloat16)
    partial_sum = jnp.dot(hidden, w_down, preferred_element_type=jnp.float32)
    summed = lax.psum(partial_sum, "blk")
    after_mlp = (rows_full.astype(jnp.float32) + summed).astype(jnp.bfloat16)
    logits = jnp.dot(rms_round(after_mlp, head_gain), w_head, preferred_element_type=jnp.float32)
    request_count = logits.shape[0]
    half_rows = request_count // 2
    slot_scale = jnp.take(guide_scale, perm)
    request_order = (
        jnp.zeros((request_count,), jnp.int32)
        .at[perm]
        .set(jnp.arange(request_count, dtype=jnp.int32))
    )
    own_order = lax.dynamic_slice_in_dim(request_order, guide_index * half_rows, half_rows)
    other_logits = partner(logits.astype(jnp.bfloat16), "guide", 0).astype(logits.dtype)
    cond_logits = jnp.where(guide_index == 0, logits, other_logits)
    uncond_logits = jnp.where(guide_index == 0, other_logits, logits)
    mixed = (uncond_logits + slot_scale[:, None] * (cond_logits - uncond_logits)).astype(
        jnp.bfloat16
    )
    return jnp.take(mixed, own_order, axis=0)


def solution(mesh):
    return jax.shard_map(
        body,
        mesh=mesh,
        in_specs=(
            P(None, "blk"),
            P("blk", None),
            P("blk", None),
            P("guide", "blk", None, None),
            P("guide", None),
            P(),
            P(),
            P(),
            P(None, "blk"),
            P(),
            P(None, "blk"),
            P(None, "blk"),
            P("blk", None),
            P(),
            P(None, "blk"),
        ),
        out_specs=P("guide", "blk"),
        check_vma=False,
    )
```

profile of v0, /device:TPU:0, one launch (start us, length us, event | category | flops | bytes accessed | tf_op | source)
XLA Modules:
  0.0 257.7 jit_solution(10083849745343940406)
XLA Ops:
  6.5 0.0 all-reduce.2.cloned.1.call-start
  6.5 1.2 reshape.73
  7.8 1.3 gather_fusion.2
  9.1 1.3 gather_fusion.3
  10.4 0.1 iota_compare_fusion
  10.5 0.7 slice_convert_fusion
  11.2 0.9 fusion.44
  12.1 2.2 fusion.55
  14.3 0.2 fusion.39
  14.5 0.1 copy.17
  14.6 2.4 fusion.4
  17.0 0.5 fusion.11
  17.5 45.3 %all_gather.6 = bf16[128,2048]{1,0:T(8,128)(2,1)S(1)} all-gather(bf16[8,2048]{1,0:T(8,128)(2,1)S(1)} %fusion.11), channel_id=1, replica_groups=mesh['guide'=2,'blk'=16] {'blk'}, dimensions={0}, use_global_device_ids=true | all-gather | bytes 557056 | tf_op jit(solution)/shard_map/all_gather | solution.py:79
  62.8 0.3 fusion.10
  63.1 38.5 %all_gather.7 = bf16[128,2048]{1,0:T(8,128)(2,1)S(1)} all-gather(bf16[128,128]{1,0:T(8,128)(2,1)S(1)} %fusion.10), channel_id=1, replica_groups=mesh['guide'=2,'blk'=16] {'blk'}, dimensions={1}, use_global_device_ids=true | all-gather | bytes 557056 | tf_op jit(solution)/shard_map/all_gather | solution.py:84
  101.7 0.2 fusion.15
  101.9 3.5 %fusion.34 = f32[128,684]{0,1:T(8,128)} fusion(bf16[2048,684]{0,1:T(8,128)(2,1)} %param.27, bf16[128,2048]{1,0:T(8,128)(2,1)S(1)} %all_gather.7, f32[2048]{0:T(1024)S(1)} %copy-done.7, f32[128]{0:T(128)S(1)} %add_rsqrt_fusion.1), kind=kOutput, calls=%fused_computation.49 | convolution fusion | flops 359661568 | bytes 3684864 | tf_op jit(solution)/shard_map/dot_general | solution.py:87
  105.4 5.0 %fusion.8 = f32[128,2048]{1,0:T(8,128)} fusion(bf16[684,2048]{1,0:T(8,128)(2,1)S(1)} %copy-done, bf16[2048,684]{0,1:T(8,128)(2,1)} %param.28, f32[128,684]{0,1:T(8,128)} %fusion.34, pred[684]{0:T(1024)(128)(4,1)S(1)} %add_compare_fusion, bf16[128,2048]{1,0:T(8,128)(2,1)S(1)} %all_gather.7, f32[2048]{0:T(1024)S(1)} %copy-done.7, f32[128]{0:T(128)S(1)} %add_rsqrt_fusion.1), kind=kOutput, calls=%fused_computation.21 | convolution fusion | flops 718887424 | bytes 7535788 | tf_op jit(solution)/shard_map/dot_general | solution.py:93
  110.4 0.0 all-reduce.2.cloned.1.call-update
  110.5 109.6 %all-reduce.2.cloned.1.call-done = f32[128,2048]{1,0:T(8,128)} async-done(((f32[128,2048]{1,0:T(8,128)}), f32[128,2048]{1,0:T(8,128)}) %all-reduce.2.cloned.1.call-update) | async-done | bytes 1048592 | tf_op jit(solution)/shard_map/psum | solution.py:94
  220.1 1.4 fusion.12
  221.5 0.0 copy-start.2
  221.5 0.0 copy-start.1
  221.5 14.7 %fusion.56 = (bf16[128,6400]{1,0:T(8,128)(2,1)}, f32[128,6400]{1,0:T(8,128)}) fusion(bf16[2048,6400]{1,0:T(8,128)(2,1)} %param.31, f32[2048]{0:T(1024)S(1)} %copy-done.5, f32[128]{0:T(128)S(1)} %add_rsqrt_fusion, f32[128,2048]{1,0:T(8,128)} %all-reduce.2.cloned.1.call-done, bf16[128,2048]{1,0:T(8,128)(2,1)S(1)} %all_gather.7), kind=kOutput, calls=%fused_computation.90 | convolution fusion | flops 3358097408 | bytes 32711168 | tf_op jit(solution)/shard_map/dot_general | solution.py:96
  236.2 0.0 collective-permute-start
  236.2 1.2 scatter_custom_fusion
  237.4 1.2 gather_fusion
  238.6 0.1 compare_and_fusion
  238.8 1.3 collective-permute-done
  240.1 4.3 %fusion.3 = bf16[128,6400]{1,0:T(8,128)(2,1)} fusion(f32[128,6400]{1,0:T(8,128)} %get-tuple-element.13, bf16[128,6400]{1,0:T(8,128)(2,1)} %collective-permute-done, f32[128]{0:T(128)S(1)} %and_select_fusion.2, pred[]{:T(512)S(6)} %eq.4), kind=kLoop, calls=%fused_computation.10 | loop fusion | flops 5734400 | bytes 6554113 | tf_op jit(solution)/shard_map/convert_element_type | solution.py:109
  244.4 4.3 %gather_fusion.1 = bf16[64,6400]{1,0:T(8,128)(2,1)} fusion(bf16[128,6400]{1,0:T(8,128)(2,1)} %fusion.3, s32[1024]{0:T(1024)S(1)} %pad_clamp_fusion), kind=kCustom, calls=%fused_computation.3 | custom fusion | bytes 1638656 | tf_op jit(solution)/shard_map/jit(_take)/gather | solution.py:112
  248.7 2.2 broadcast_select_fusion
  (29 shorter events, 0.1 us)
Async XLA Ops:
  6.5 98.9 %copy-start = (bf16[684,2048]{1,0:T(8,128)(2,1)S(1)}, bf16[684,2048]{1,0:T(8,128)(2,1)}, u32[]{:S(2)}) copy-start(bf16[684,2048]{1,0:T(8,128)(2,1)} %param.29) | copy-start | bytes 8404996
  6.5 213.5 %all-reduce.2.cloned.1.call-start = ((), (), s32[]{:S(2)}) async-start(), calls=%async_computation | async-start | bytes 2097152 | tf_op jit(solution)/shard_map/psum | solution.py:94
  14.6 2.4 copy-start.3
  14.6 48.3 %copy-start.4 = (bf16[2048,128]{1,0:T(8,128)(2,1)S(1)}, bf16[2048,128]{1,0:T(8,128)(2,1)}, u32[]{:S(2)}) copy-start(bf16[2048,128]{1,0:T(8,128)(2,1)} %param.25) | copy-start | bytes 1572868
  14.6 48.3 %copy-start.6 = (bf16[128,128]{1,0:T(8,128)(2,1)S(1)}, bf16[128,128]{1,0:T(8,128)(2,1)}, u32[]{:S(2)}) copy-start(bf16[128,128]{1,0:T(8,128)(2,1)} %param.17) | copy-start | bytes 98308
  17.0 84.9 %copy-start.7 = (f32[2048]{0:T(1024)S(1)}, f32[2048]{0:T(1024)}, u32[]{:S(2)}) copy-start(f32[2048]{0:T(1024)} %param.26) | copy-start | bytes 24580
  105.4 116.1 %copy-start.5 = (f32[2048]{0:T(1024)S(1)}, f32[2048]{0:T(1024)}, u32[]{:S(2)}) copy-start(f32[2048]{0:T(1024)} %param.30) | copy-start | bytes 24580
  221.5 14.7 %copy-start.2 = (s32[128]{0:T(128)S(1)}, s32[128]{0:T(128)}, u32[]{:S(2)}) copy-start(s32[128]{0:T(128)} %param.22) | copy-start | bytes 1540
  221.5 15.9 %copy-start.1 = (f32[128]{0:T(128)S(1)}, f32[128]{0:T(128)}, u32[]{:S(2)}) copy-start(f32[128]{0:T(128)} %param.23) | copy-start | bytes 1540
  236.2 3.8 %collective-permute-start = (bf16[128,6400]{1,0:T(8,128)(2,1)}, bf16[128,6400]{1,0:T(8,128)(2,1)}, u32[]{:S(2)}, u32[]{:S(2)}) collective-permute-start(bf16[128,6400]{1,0:T(8,128)(2,1)} %get-tuple-element.12), channel_id=1, source_target_pairs={{0,16},{16,0},{1,17},{17,1},{2,18},{18,2},{3,19},{19,3},{4,20},{20... | collective-permute-start | bytes 4915208 | tf_op jit(solution)/shard_map/ppermute | solution.py:12
Sparse Core Ops, SparseCore 0:
  110.6 109.4 all-reduce.1
where the time goes:
time: 258 us
  waiting for transfers between devices  111 us (43%)
  blocking collectives  83.9 us (33%)
  matrix products  29.5 us (11%)
  between operations  13.5 us (5%)
  local copies, waits for them, and re-layouts  10.7 us (4%)
  other arithmetic  9.26 us (4%)
    psum x1, waiting for transfers between devices, body(): summed = lax.psum(partial_sum, 'blk')  110 us
    all_gather x1, blocking collectives, body(): lax.all_gather(value_rows, 'blk', axis=0, tiled=True)  45.3 us
    all_gather x1, blocking collectives, body(): rows_full = lax.all_gather(residual, 'blk', axis=1, tiled=True)  38.5 us
    dot_general x1, matrix products, body(): jnp.dot(rms_round(after_mlp, head_gain), w_head, preferred_element_type=j...  14.7 us
  transfers between devices with their start and end apart: 2, of which 2 were waited for; matrix products, arithmetic and copies ran while one was open for 1% of the time, Pallas kernels for 0%

commit v1 on v0

--- a/solution.py
+++ b/solution.py
@@ -4,6 +4,18 @@
 from jax.sharding import PartitionSpec as P
 
 FF = 10944
+
+
+def gather_by_bits(x, axis, dim):
+    ways, here = (lax.axis_size(axis), lax.axis_index(axis))
+    grown, reach = (x, 1)
+    while reach < ways:
+        theirs = lax.ppermute(grown, axis, [(d, d ^ reach) for d in range(ways)])
+        mine_first = jnp.concatenate([grown, theirs], axis=dim)
+        theirs_first = jnp.concatenate([theirs, grown], axis=dim)
+        grown = jnp.where(here & reach == 0, mine_first, theirs_first)
+        reach = 2 * reach
+    return grown
 
 
 def partner(value, axis, apart):
@@ -76,9 +88,7 @@
     )
     value_rows = value_rows.astype(jnp.bfloat16).reshape(slots_dev, -1)
     attended = jnp.dot(
-        lax.all_gather(value_rows, "blk", axis=0, tiled=True),
-        w_out,
-        preferred_element_type=jnp.float32,
+        gather_by_bits(value_rows, "blk", 0), w_out, preferred_element_type=jnp.float32
     )
     residual = (x_cols.astype(jnp.float32) + attended).astype(jnp.bfloat16)
     rows_full = lax.all_gather(residual, "blk", axis=1, tiled=True)

time: 258 us -> 242 us (0.938)
  blocking collectives: 83.9 us -> 43.7 us
  waiting for transfers between devices: 111 us -> 124 us
  starting transfers between devices: 0.01 us -> 11.5 us
    all_gather x1 -> x0, blocking collectives: 45.3 us -> none  [body(): lax.all_gather(value_rows, 'blk', axis=0, tiled=True)]
    ppermute x0 -> x4, waiting for transfers between devices: none -> 14.6 us  [gather_by_bits(): theirs = lax.ppermute(grown, axis, [(d, d ^ reach) for d in range(ways)])]
    ppermute x0 -> x4, starting transfers between devices: none -> 11.5 us  [gather_by_bits(): theirs = lax.ppermute(grown, axis, [(d, d ^ reach) for d in range(ways)])]
    all_gather x1, blocking collectives: 38.5 us -> 43.7 us  [body(): rows_full = lax.all_gather(residual, 'blk', axis=1, tiled=True)]
  transfers between devices with their start and end apart: 2 -> 6, of which waited for: 2 -> 6; matrix products, arithmetic and copies ran while one was open for 1% -> 1% of each run, Pallas kernels for 0% -> 0%
where the time goes in v1:
time: 242 us; the launch traced here: 241 us
  waiting for transfers between devices  124 us (51%)
  blocking collectives  43.7 us (18%)
  matrix products  28.9 us (12%)
  between operations  13.6 us (6%)
  starting transfers between devices  11.5 us (5%)
  local copies, waits for them, and re-layouts  10.7 us (4%)
  other arithmetic  9.36 us (4%)
    psum x1, waiting for transfers between devices, body(): summed = lax.psum(partial_sum, 'blk')  108 us
    all_gather x1, blocking collectives, body(): rows_full = lax.all_gather(residual, 'blk', axis=1, tiled=True)  43.7 us
    dot_general x1, matrix products, body(): jnp.dot(rms_round(after_mlp, head_gain), w_head, preferred_element_type=j...  14.7 us
    ppermute x4, waiting for transfers between devices, gather_by_bits(): theirs = lax.ppermute(grown, axis, [(d, d ^ reach) for d in range(ways)])  14.6 us
    ppermute x4, starting transfers between devices, gather_by_bits(): theirs = lax.ppermute(grown, axis, [(d, d ^ reach) for d in range(ways)])  11.5 us
    dot_general x1, matrix products, body(): partial_sum = jnp.dot(hidden, w_down, preferred_element_type=jnp.float32)  5.04 us
  transfers between devices with their start and end apart: 6, of which 6 were waited for; matrix products, arithmetic and copies ran while one was open for 1% of the time, Pallas kernels for 0%

profile of v1, /device:TPU:0, one launch (start us, length us, event | category | flops | bytes accessed | tf_op | source)
XLA Modules:
  0.0 241.3 jit_solution(14094927562323134686)
XLA Ops:
  6.5 1.2 reshape.73
  7.8 1.3 gather_fusion.2
  9.1 1.3 gather_fusion.3
  10.5 0.7 slice_convert_fusion
  11.2 0.9 fusion.50
  12.1 2.2 fusion.62
  14.3 0.2 fusion.45
  14.6 2.4 fusion.4
  17.0 0.5 fusion.11
  17.5 3.0 %collective-permute-start = (bf16[8,2048]{1,0:T(8,128)(2,1)S(1)}, bf16[8,2048]{1,0:T(8,128)(2,1)S(1)}, u32[]{:S(2)}, u32[]{:S(2)}) collective-permute-start(bf16[8,2048]{1,0:T(8,128)(2,1)S(1)} %fusion.11), channel_id=1, source_target_pairs={{0,1},{1,0},{2,3},{3,2},{4,5},{5,4},{6,7},{7,6},{8,9},{9,8},{10,11... | collective-permute-start | bytes 98312 | tf_op jit(solution)/shard_map/ppermute | solution.py:13
  20.5 1.9 collective-permute-done
  22.4 2.1 collective-permute-start.1
  24.5 2.2 collective-permute-done.1
  26.8 2.1 collective-permute-start.2
  28.9 2.9 %collective-permute-done.2 = bf16[32,2048]{1,0:T(8,128)(2,1)S(1)} collective-permute-done((bf16[32,2048]{1,0:T(8,128)(2,1)S(1)}, bf16[32,2048]{1,0:T(8,128)(2,1)S(1)}, u32[]{:S(2)}, u32[]{:S(2)}) %collective-permute-start.2) | collective-permute-done | bytes 131104 | tf_op jit(solution)/shard_map/ppermute | solution.py:13
  31.9 4.2 %collective-permute-start.3 = (bf16[64,2048]{1,0:T(8,128)(2,1)S(1)}, bf16[64,2048]{1,0:T(8,128)(2,1)}, u32[]{:S(2)}, u32[]{:S(2)}) collective-permute-start(bf16[64,2048]{1,0:T(8,128)(2,1)S(1)} %maximum_select_fusion.2), channel_id=1, source_target_pairs={{0,8},{1,9},{2,10},{3,11},{4,12},{5,13},{6,14},{7,15},{8,0},{9,1},... | collective-permute-start | bytes 786440 | tf_op jit(solution)/shard_map/ppermute | solution.py:13
  36.1 7.5 %collective-permute-done.3 = bf16[64,2048]{1,0:T(8,128)(2,1)} collective-permute-done((bf16[64,2048]{1,0:T(8,128)(2,1)S(1)}, bf16[64,2048]{1,0:T(8,128)(2,1)}, u32[]{:S(2)}, u32[]{:S(2)}) %collective-permute-start.3) | collective-permute-done | bytes 262176 | tf_op jit(solution)/shard_map/ppermute | solution.py:13
  43.6 1.5 fusion.10
  45.1 43.7 %all_gather.3 = bf16[128,2048]{1,0:T(8,128)(2,1)S(1)} all-gather(bf16[128,128]{1,0:T(8,128)(2,1)S(1)} %fusion.10), channel_id=1, replica_groups=mesh['guide'=2,'blk'=16] {'blk'}, dimensions={1}, use_global_device_ids=true | all-gather | bytes 557056 | tf_op jit(solution)/shard_map/all_gather | solution.py:94
  88.8 0.2 fusion.15
  89.0 1.7 fusion.40
  90.7 5.0 %fusion.8 = f32[128,2048]{1,0:T(8,128)} fusion(bf16[684,2048]{1,0:T(8,128)(2,1)S(1)} %copy-done, bf16[2048,684]{0,1:T(8,128)(2,1)} %param.28, f32[128,684]{0,1:T(8,128)} %fusion.40, pred[684]{0:T(1024)(128)(4,1)S(1)} %add_compare_fusion, bf16[128,2048]{1,0:T(8,128)(2,1)S(1)} %all_gather.3, f32[2048]{0:T(1024)S(1)} %copy-done.6, f32[128]{0:T(128)S(1)} %add_rsqrt_fusion.1), kind=kOutput, calls=%fused_computation.21 | convolution fusion | flops 718887424 | bytes 7535788 | tf_op jit(solution)/shard_map/dot_general | solution.py:103
  95.8 107.8 %all-reduce.2.cloned.1.call-done = f32[128,2048]{1,0:T(8,128)} async-done(((f32[128,2048]{1,0:T(8,128)}), f32[128,2048]{1,0:T(8,128)}) %all-reduce.2.cloned.1.call-update) | async-done | bytes 1048592 | tf_op jit(solution)/shard_map/psum | solution.py:104
  203.6 1.5 fusion.12
  205.1 14.7 %fusion.63 = (bf16[128,6400]{1,0:T(8,128)(2,1)}, f32[128,6400]{1,0:T(8,128)}) fusion(bf16[2048,6400]{1,0:T(8,128)(2,1)} %param.31, f32[2048]{0:T(1024)S(1)} %copy-done.5, f32[128]{0:T(128)S(1)} %add_rsqrt_fusion, f32[128,2048]{1,0:T(8,128)} %all-reduce.2.cloned.1.call-done, bf16[128,2048]{1,0:T(8,128)(2,1)S(1)} %all_gather.3), kind=kOutput, calls=%fused_computation.101 | convolution fusion | flops 3358097408 | bytes 32711168 | tf_op jit(solution)/shard_map/dot_general | solution.py:106
  219.8 1.2 scatter_custom_fusion
  220.9 1.2 gather_fusion
  222.2 0.1 compare_and_fusion
  222.3 1.3 collective-permute-done.4
  223.6 4.3 %fusion.3 = bf16[128,6400]{1,0:T(8,128)(2,1)} fusion(f32[128,6400]{1,0:T(8,128)} %get-tuple-element.13, bf16[128,6400]{1,0:T(8,128)(2,1)} %collective-permute-done.4, f32[128]{0:T(128)S(1)} %and_select_fusion.2, pred[]{:T(512)S(6)} %eq.16), kind=kLoop, calls=%fused_computation.10 | loop fusion | flops 5734400 | bytes 6554113 | tf_op jit(solution)/shard_map/convert_element_type | solution.py:119
  227.9 4.3 %gather_fusion.1 = bf16[64,6400]{1,0:T(8,128)(2,1)} fusion(bf16[128,6400]{1,0:T(8,128)(2,1)} %fusion.3, s32[1024]{0:T(1024)S(1)} %pad_clamp_fusion), kind=kCustom, calls=%fused_computation.3 | custom fusion | bytes 1638656 | tf_op jit(solution)/shard_map/jit(_take)/gather | solution.py:122
  232.2 2.2 broadcast_select_fusion
  (39 shorter events, 0.4 us)
Async XLA Ops:
  6.5 84.2 %copy-start = (bf16[684,2048]{1,0:T(8,128)(2,1)S(1)}, bf16[684,2048]{1,0:T(8,128)(2,1)}, u32[]{:S(2)}) copy-start(bf16[684,2048]{1,0:T(8,128)(2,1)} %param.29) | copy-start | bytes 8404996
  6.5 197.0 %all-reduce.2.cloned.1.call-start = ((), (), s32[]{:S(2)}) async-start(), calls=%async_computation | async-start | bytes 2097152 | tf_op jit(solution)/shard_map/psum | solution.py:104
  14.6 2.4 copy-start.4
  14.6 29.0 %copy-start.7 = (bf16[128,128]{1,0:T(8,128)(2,1)S(1)}, bf16[128,128]{1,0:T(8,128)(2,1)}, u32[]{:S(2)}) copy-start(bf16[128,128]{1,0:T(8,128)(2,1)} %param.17) | copy-start | bytes 98308
  17.5 71.5 %copy-start.6 = (f32[2048]{0:T(1024)S(1)}, f32[2048]{0:T(1024)}, u32[]{:S(2)}) copy-start(f32[2048]{0:T(1024)} %param.26) | copy-start | bytes 24580
  17.5 4.9 %collective-permute-start = (bf16[8,2048]{1,0:T(8,128)(2,1)S(1)}, bf16[8,2048]{1,0:T(8,128)(2,1)S(1)}, u32[]{:S(2)}, u32[]{:S(2)}) collective-permute-start(bf16[8,2048]{1,0:T(8,128)(2,1)S(1)} %fusion.11), channel_id=1, source_target_pairs={{0,1},{1,0},{2,3},{3,2},{4,5},{5,4},{6,7},{7,6},{8,9},{9,8},{10,11... | collective-permute-start | bytes 98312 | tf_op jit(solution)/shard_map/ppermute | solution.py:13
  22.4 4.4 %collective-permute-start.1 = (bf16[16,2048]{1,0:T(8,128)(2,1)S(1)}, bf16[16,2048]{1,0:T(8,128)(2,1)S(1)}, u32[]{:S(2)}, u32[]{:S(2)}) collective-permute-start(bf16[16,2048]{1,0:T(8,128)(2,1)S(1)} %maximum_select_fusion.4), channel_id=1, source_target_pairs={{0,2},{1,3},{2,0},{3,1},{4,6},{5,7},{6,4},{7,5},{8,10},{9,11},{10,... | collective-permute-start | bytes 196616 | tf_op jit(solution)/shard_map/ppermute | solution.py:13
  26.8 5.1 %collective-permute-start.2 = (bf16[32,2048]{1,0:T(8,128)(2,1)S(1)}, bf16[32,2048]{1,0:T(8,128)(2,1)S(1)}, u32[]{:S(2)}, u32[]{:S(2)}) collective-permute-start(bf16[32,2048]{1,0:T(8,128)(2,1)S(1)} %maximum_select_fusion.3), channel_id=1, source_target_pairs={{0,4},{1,5},{2,6},{3,7},{4,0},{5,1},{6,2},{7,3},{8,12},{9,13},{10,... | collective-permute-start | bytes 393224 | tf_op jit(solution)/shard_map/ppermute | solution.py:13
  31.9 11.7 %collective-permute-start.3 = (bf16[64,2048]{1,0:T(8,128)(2,1)S(1)}, bf16[64,2048]{1,0:T(8,128)(2,1)}, u32[]{:S(2)}, u32[]{:S(2)}) collective-permute-start(bf16[64,2048]{1,0:T(8,128)(2,1)S(1)} %maximum_select_fusion.2), channel_id=1, source_target_pairs={{0,8},{1,9},{2,10},{3,11},{4,12},{5,13},{6,14},{7,15},{8,0},{9,1},... | collective-permute-start | bytes 786440 | tf_op jit(solution)/shard_map/ppermute | solution.py:13
  36.1 52.9 %copy-start.3 = (bf16[2048,684]{0,1:T(8,128)(2,1)S(1)}, bf16[2048,684]{0,1:T(8,128)(2,1)}, u32[]{:S(2)}) copy-start(bf16[2048,684]{0,1:T(8,128)(2,1)} %param.27) | copy-start | bytes 8404996
  90.7 114.3 %copy-start.5 = (f32[2048]{0:T(1024)S(1)}, f32[2048]{0:T(1024)}, u32[]{:S(2)}) copy-start(f32[2048]{0:T(1024)} %param.30) | copy-start | bytes 24580
  205.1 14.7 %copy-start.2 = (s32[128]{0:T(128)S(1)}, s32[128]{0:T(128)}, u32[]{:S(2)}) copy-start(s32[128]{0:T(128)} %param.22) | copy-start | bytes 1540
  205.1 15.9 %copy-start.1 = (f32[128]{0:T(128)S(1)}, f32[128]{0:T(128)}, u32[]{:S(2)}) copy-start(f32[128]{0:T(128)} %param.23) | copy-start | bytes 1540
  219.7 3.8 %collective-permute-start.4 = (bf16[128,6400]{1,0:T(8,128)(2,1)}, bf16[128,6400]{1,0:T(8,128)(2,1)}, u32[]{:S(2)}, u32[]{:S(2)}) collective-permute-start(bf16[128,6400]{1,0:T(8,128)(2,1)} %get-tuple-element.12), channel_id=1, source_target_pairs={{0,16},{16,0},{1,17},{17,1},{2,18},{18,2},{3,19},{19,3},{4,20},{20... | collective-permute-start | bytes 4915208 | tf_op jit(solution)/shard_map/ppermute | solution.py:24
Sparse Core Ops, SparseCore 0:
  95.9 107.6 all-reduce.1
